TPU v7x, 32 devices: a whole 2x2x4 slice. The times are simulated.
32 devices in a mesh: row: 4 (over y, x), col: 8 (over z, core).
Axes of the slice: x: 2, y: 2, z: 4, core: 2. Of those that a mesh axis runs over, the one named last changes fastest.
Arguments:
- sim: bfloat16 [8192, 8192], P('row', 'col'), may hold values from -6 to 6
- diag_blocks: bfloat16 [2048, 8192], P(None, 'col'), may hold values from -0.125 to 0.125
- match_perm: int32 [4, 2048], replicated, may hold values from 0 to 2047, each once within a row
- match_scale: float32 [4, 2048], replicated, may hold values from 0.3 to 1.5
- features: bfloat16 [8192, 256], P('col'), may hold values from -0.0625 to 0.0625
Outputs:
- new_sim: bfloat16 [8192, 8192], P('row', 'col')
- aggregated: float32 [8192, 256], P(('row', 'col'))
Inputs may be any that keep to these rules, and one draw needn't show every extreme that they name: Each row of match_perm lists every number of 0 to 2047 once.
All inputs are finite; a program needn't handle non-finite values.
Results may differ from a plain program's by a relative error of at most 0.0058.
Values may be sent and summed in bfloat16 or wider, within the bound.
No kernel may reach another device: no remote copies, remote signals or barrier semaphores. Data moves between devices by JAX's collectives and lax.ppermute only.
A program may use at most 128 MiB of HBM per device.

v0:
```python
import jax
import jax.numpy as jnp
from jax import lax
from jax.sharding import PartitionSpec as P

decay_factor = 0.8


def partner_2(value, axis, bit):
    mask = 2**bit
    pairs = [(source, source ^ mask) for source in range(lax.axis_size(axis))]
    return lax.ppermute(value, axis, pairs)


def shifted(value, axis, steps):
    count = lax.axis_size(axis)
    pairs = [(source, (source + steps) % count) for source in range(count)]
    return lax.ppermute(value, axis, pairs)


def spread(x, axis, root):
    mine = lax.axis_index(axis) == root
    return lax.psum(jnp.where(mine, x, jnp.zeros_like(x)), axis)


def on_device(sim, diag_blocks, match_perm, match_scale, features):
    row_count = lax.axis_size("row")
    col_count = lax.axis_size("col")
    blocks_here = col_count // 2 // row_count
    row_id = lax.axis_index("row")
    col_id = lax.axis_index("col")
    block_id = col_id // 2
    side = col_id % 2
    half_width = sim.shape[1]
    tile_rows = sim.shape[0]
    partner = partner_2(sim, "col", 0)
    first_half = jnp.where(side == 0, sim, partner)
    second_half = jnp.where(side == 0, partner, sim)
    whole_block = jnp.concatenate([first_half, second_half], axis=1)
    perm_block = lax.dynamic_index_in_dim(match_perm, block_id, 0, keepdims=False)
    scale_block = lax.dynamic_index_in_dim(match_scale, block_id, 0, keepdims=False)
    own_perm = lax.dynamic_slice_in_dim(perm_block, side * half_width, half_width, 0)
    own_scale = lax.dynamic_slice_in_dim(scale_block, side * half_width, half_width, 0)
    moved_cols = (jnp.take(whole_block, own_perm, axis=1) * own_scale[None, :]).astype(jnp.bfloat16)
    arrived_cols = shifted(moved_cols, "col", col_count // 2)
    mixed = (
        jnp.dot(whole_block, diag_blocks, preferred_element_type=jnp.float32) + arrived_cols
    ).astype(jnp.bfloat16)
    position = 0
    source = row_id * blocks_here + position
    perm_rows = lax.dynamic_index_in_dim(match_perm, source, 0, keepdims=False)
    scale_rows = lax.dynamic_index_in_dim(match_scale, source, 0, keepdims=False)
    sent_rows = (jnp.take(mixed, perm_rows, axis=0) * scale_rows[:, None]).astype(jnp.bfloat16)
    arrived_rows = shifted(sent_rows, "row", row_count // 2)
    position = 0
    target = row_id * blocks_here + position
    halves = []
    for part in range(2):
        left_half = spread(diag_blocks, "col", 2 * target + part)
        halves.append(
            lax.dot_general(
                left_half, mixed, (((0,), (0,)), ((), ())), preferred_element_type=jnp.float32
            )
        )
    product = jnp.concatenate(halves, axis=0)
    results = decay_factor * (product + arrived_rows)
    global_rows = row_id * tile_rows + lax.broadcasted_iota(jnp.int32, results.shape, 0)
    global_cols = col_id * half_width + lax.broadcasted_iota(jnp.int32, results.shape, 1)
    new_sim = jnp.where(global_rows == global_cols, 1.0, results).astype(jnp.bfloat16)
    partial_value = jnp.dot(new_sim, features, preferred_element_type=jnp.float32)
    aggregated = lax.psum_scatter(partial_value, "col", scatter_dimension=0, tiled=True)
    return (new_sim, aggregated)


def solution(mesh):
    placed = (P("row", "col"), P(None, "col"), P(), P(), P("col", None))
    return jax.shard_map(
        on_device,
        mesh=mesh,
        in_specs=placed,
        out_specs=(P("row", "col"), P(("row", "col"), None)),
        check_vma=False,
    )
```

profile of v0, /device:TPU:0, one launch (start us, length us, event | category | flops | bytes accessed | tf_op | source)
XLA Modules:
  0.0 503.9 jit_solution(8184790162820065224)
XLA Ops:
  7.2 0.0 copy-start
  7.2 0.0 all-reduce.3.cloned.1.call-start
  7.2 6.5 %copy.12 = bf16[2048,1024]{0,1:T(8,128)(2,1)} copy(bf16[2048,1024]{1,0:T(8,128)(2,1)} %param.5) | data formatting | bytes 8388608 | tf_op args[0]
  13.7 0.5 collective-permute-start
  14.2 0.8 dynamic_slice.23
  15.0 0.8 compare_select_fusion.1
  15.8 5.5 %collective-permute-done = bf16[2048,1024]{0,1:T(8,128)(2,1)} collective-permute-done((bf16[2048,1024]{0,1:T(8,128)(2,1)}, bf16[2048,1024]{0,1:T(8,128)(2,1)}, u32[]{:S(2)}, u32[]{:S(2)}) %collective-permute-start) | collective-permute-done | bytes 4194336 | tf_op jit(solution)/shard_map/ppermute | solution.py:12
  21.3 5.7 %broadcast_select_fusion.2 = (bf16[2048,1024]{0,1:T(8,128)(2,1)}, bf16[2048,1024]{0,1:T(8,128)(2,1)}) fusion(bf16[2048,1024]{0,1:T(8,128)(2,1)} %copy.12, bf16[2048,1024]{0,1:T(8,128)(2,1)} %collective-permute-done, pred[]{:T(512)S(6)} %eq.17), kind=kLoop, calls=%fused_computation.13 | loop fusion | flops 4194304 | bytes 16777216 | tf_op jit(solution)/shard_map/jit(_where)/select_n | solution.py:37
  27.0 8.4 %pad_maximum_fusion = bf16[2048,2048]{0,1:T(8,128)(2,1)} fusion(bf16[2048,1024]{0,1:T(8,128)(2,1)} %get-tuple-element.9, bf16[2048,1024]{0,1:T(8,128)(2,1)} %get-tuple-element.8), kind=kLoop, calls=%fused_computation.2 | loop fusion | flops 16777216 | bytes 16777216 | tf_op jit(solution)/shard_map/concatenate | solution.py:39
  35.4 13.3 %gather_fusion = bf16[1024,2048]{1,0:T(8,128)(2,1)} fusion(bf16[2048,2048]{0,1:T(8,128)(2,1)} %pad_maximum_fusion, s32[1024]{0:T(1024)S(1)} %broadcast_clamp_fusion.1), kind=kCustom, calls=%fused_computation | custom fusion | bytes 8392704 | tf_op jit(solution)/shard_map/jit(_take)/gather | solution.py:44
  48.7 6.4 %copy.14 = bf16[1024,2048]{0,1:T(8,128)(2,1)} copy(bf16[1024,2048]{1,0:T(8,128)(2,1)} %gather_fusion) | data formatting | bytes 8388608 | tf_op jit(solution)/shard_map/jit(_take)/gather | solution.py:44
  55.1 5.4 %fusion.3 = bf16[2048,1024]{1,0:T(8,128)(2,1)} fusion(f32[1024]{0:T(1024)S(1)} %bitcast.22, bf16[1024,2048]{0,1:T(8,128)(2,1)} %copy.14, pred[1024]{0:T(1024)(128)(4,1)S(1)} %compare_and_fusion.1), kind=kLoop, calls=%fused_computation.10 | loop fusion | flops 8388608 | bytes 8393728 | tf_op jit(solution)/shard_map/convert_element_type | solution.py:44
  60.4 3.9 collective-permute-start.1
  64.4 6.0 %broadcast_select_fusion.3 = (bf16[2048,1024]{1,0:T(8,128)(2,1)}, bf16[2048,1024]{1,0:T(8,128)(2,1)}) fusion(bf16[2048,1024]{1,0:T(8,128)(2,1)} %param.6, pred[]{:T(512)S(6)} %eq.16, pred[]{:T(512)S(6)} %eq.18), kind=kLoop, calls=%fused_computation.14 | loop fusion | flops 4194304 | bytes 12582914 | tf_op jit(solution)/shard_map/jit(_where)/select_n | solution.py:23
  70.4 0.0 all-reduce.3.cloned.1.call-update
  70.5 0.2 reduce-scatter.2.cloned.1.call-start
  70.7 0.8 constant_dynamic-slice_fusion
  71.5 0.8 compare_select_fusion
  72.3 251.8 %collective-permute-done.1 = bf16[2048,1024]{1,0:T(8,128)(2,1)} collective-permute-done((bf16[2048,1024]{1,0:T(8,128)(2,1)}, bf16[2048,1024]{1,0:T(8,128)(2,1)}, u32[]{:S(2)}, u32[]{:S(2)}) %collective-permute-start.1) | collective-permute-done | bytes 4194336 | tf_op jit(solution)/shard_map/ppermute | solution.py:18
  324.1 14.7 %add_convert_fusion = bf16[2048,1024]{1,0:T(8,128)(2,1)} fusion(bf16[2048,1024]{1,0:T(8,128)(2,1)} %collective-permute-done.1, bf16[2048,1024]{1,0:T(8,128)(2,1)} %param.6, bf16[2048,1024]{0,1:T(8,128)(2,1)} %get-tuple-element.9, bf16[2048,1024]{0,1:T(8,128)(2,1)} %get-tuple-element.8), kind=kOutput, calls=%fused_computation.9 | convolution fusion | flops 8613003264 | bytes 20971520 | tf_op jit(solution)/shard_map/dot_general | solution.py:47
  338.8 13.7 %gather_fusion.1 = bf16[2048,1024]{1,0:T(8,128)(2,1)} fusion(bf16[2048,1024]{1,0:T(8,128)(2,1)} %add_convert_fusion, s32[2048]{0:T(1024)S(1)} %broadcast_clamp_fusion), kind=kCustom, calls=%fused_computation.1 | custom fusion | bytes 8396800 | tf_op jit(solution)/shard_map/jit(_take)/gather | solution.py:53
  352.5 4.2 multiply_convert_fusion.1
  356.7 1.6 collective-permute-start.2
  358.3 44.8 %all-reduce.3.cloned.1.call-done = (bf16[2048,1024]{1,0:T(8,128)(2,1)}, bf16[2048,1024]{1,0:T(8,128)(2,1)}) async-done(((bf16[2048,1024]{1,0:T(8,128)(2,1)}, bf16[2048,1024]{1,0:T(8,128)(2,1)}), (bf16[2048,1024]{1,0:T(8,128)(2,1)}, bf16[2048,1024]{1,0:T(8,128)(2,1)})) %all-reduce.3.cloned.1.call-update) | async-done | bytes 8388624 | tf_op jit(solution)/shard_map/psum | solution.py:23
  403.1 0.0 copy-start.1
  403.1 0.0 copy-start.3
  403.2 7.9 %fusion.4 = f32[1024,1024]{1,0:T(8,128)S(1)} fusion(bf16[2048,1024]{1,0:T(8,128)(2,1)} %get-tuple-element.3, bf16[2048,1024]{1,0:T(8,128)(2,1)} %add_convert_fusion), kind=kOutput, calls=%fused_computation.27 | convolution fusion | flops 4294967296 | bytes 12582912 | tf_op jit(solution)/shard_map/dot_general | solution.py:61
  411.1 0.0 copy-done.1
  411.1 0.0 copy-done.3
  411.1 4.6 fusion.5
  415.8 33.4 %collective-permute-done.2 = bf16[2048,1024]{1,0:T(8,128)(2,1)} collective-permute-done((bf16[2048,1024]{1,0:T(8,128)(2,1)}, bf16[2048,1024]{1,0:T(8,128)(2,1)}, u32[]{:S(2)}, u32[]{:S(2)}) %collective-permute-start.2) | collective-permute-done | bytes 4194336 | tf_op jit(solution)/shard_map/ppermute | solution.py:18
  449.1 4.1 fusion.2
  453.3 0.0 copy-start.2
  453.3 2.0 copy-done.2
  455.3 0.0 copy-done
  455.3 2.6 fusion.6
  457.9 0.0 reduce-scatter.2.cloned.1.call-update
  457.9 39.2 %reduce-scatter.2.cloned.1.call-done = f32[256,256]{1,0:T(8,128)} async-done(((f32[2048,256]{1,0:T(8,128)}), f32[256,256]{1,0:T(8,128)}) %reduce-scatter.2.cloned.1.call-update) | async-done | bytes 262160 | tf_op jit(solution)/shard_map/reduce_scatter | solution.py:71
  (6 shorter events, 0.0 us)
Async XLA Ops:
  7.2 448.1 %copy-start = (bf16[1024,256]{1,0:T(8,128)(2,1)S(1)}, bf16[1024,256]{1,0:T(8,128)(2,1)}, u32[]{:S(2)}) copy-start(bf16[1024,256]{1,0:T(8,128)(2,1)} %param.9) | copy-start | bytes 1572868
  7.2 396.0 %all-reduce.3.cloned.1.call-start = ((), (), s32[]{:S(2)}) async-start(), calls=%async_computation.2 | async-start | bytes 16777216 | tf_op jit(solution)/shard_map/psum | solution.py:23
  13.7 7.6 %collective-permute-start = (bf16[2048,1024]{0,1:T(8,128)(2,1)}, bf16[2048,1024]{0,1:T(8,128)(2,1)}, u32[]{:S(2)}, u32[]{:S(2)}) collective-permute-start(bf16[2048,1024]{0,1:T(8,128)(2,1)} %copy.12), channel_id=1, source_target_pairs={{0,1},{1,0},{2,3},{3,2},{4,5},{5,4},{6,7},{7,6},{8,9},{9,8},{10,11... | collective-permute-start | bytes 12582920 | tf_op jit(solution)/shard_map/ppermute | solution.py:12
  60.4 263.7 %collective-permute-start.1 = (bf16[2048,1024]{1,0:T(8,128)(2,1)}, bf16[2048,1024]{1,0:T(8,128)(2,1)}, u32[]{:S(2)}, u32[]{:S(2)}) collective-permute-start(bf16[2048,1024]{1,0:T(8,128)(2,1)} %fusion.3), channel_id=1, source_target_pairs={{0,4},{1,5},{2,6},{3,7},{4,0},{5,1},{6,2},{7,3},{8,12},{9,13},{10,... | collective-permute-start | bytes 12582920 | tf_op jit(solution)/shard_map/ppermute | solution.py:18
  70.5 426.6 %reduce-scatter.2.cloned.1.call-start = ((), (), s32[]{:S(2)}) async-start(), calls=%async_computation.1 | async-start | bytes 2359296 | tf_op jit(solution)/shard_map/reduce_scatter | solution.py:71
  356.7 92.5 %collective-permute-start.2 = (bf16[2048,1024]{1,0:T(8,128)(2,1)}, bf16[2048,1024]{1,0:T(8,128)(2,1)}, u32[]{:S(2)}, u32[]{:S(2)}) collective-permute-start(bf16[2048,1024]{1,0:T(8,128)(2,1)} %multiply_convert_fusion.1), channel_id=1, source_target_pairs={{0,16},{8,24},{16,0},{24,8},{1,17},{9,25},{17,1},{25,9},{2,18},{10... | collective-permute-start | bytes 12582920 | tf_op jit(solution)/shard_map/ppermute | solution.py:18
  403.1 8.0 %copy-start.1 = (bf16[2048,1024]{1,0:T(8,128)(2,1)S(1)}, bf16[2048,1024]{1,0:T(8,128)(2,1)}, u32[]{:S(2)}) copy-start(bf16[2048,1024]{1,0:T(8,128)(2,1)} %add_convert_fusion) | copy-start | bytes 12582916
  403.1 8.0 %copy-start.3 = (bf16[2048,1024]{1,0:T(8,128)(2,1)S(1)}, bf16[2048,1024]{1,0:T(8,128)(2,1)}, u32[]{:S(2)}) copy-start(bf16[2048,1024]{1,0:T(8,128)(2,1)} %get-tuple-element.2) | copy-start | bytes 12582916
  453.3 2.0 copy-start.2
Sparse Core Ops, SparseCore 0:
  70.6 332.5 all-reduce.2
  458.0 38.9 reduce-scatter.1
where the time goes:
time: 505 us; the launch traced here: 504 us
  waiting for transfers between devices  375 us (74%)
  local copies, waits for them, and re-layouts  43.5 us (9%)
  other arithmetic  35.4 us (7%)
  matrix products  29.8 us (6%)
  between operations  14.1 us (3%)
  starting transfers between devices  6.31 us (1%)
    ppermute x2, waiting for transfers between devices, shifted(): return lax.ppermute(value, axis, pairs)  285 us
    psum x1, waiting for transfers between devices, spread(): return lax.psum(jnp.where(mine, x, jnp.zeros_like(x)), axis)  44.8 us
    reduce_scatter x1, waiting for transfers between devices, on_device(): lax.psum_scatter(partial_value, 'col', scatter_dimension=0, tiled=True)  39.2 us
    gather x2, local copies, waits for them, and re-layouts, on_device(): jnp.take(whole_block, own_perm, axis=1) * own_scale[None, :]  19.7 us
    dot_general x1, matrix products, on_device(): jnp.dot(whole_block, diag_blocks, preferred_element_type=jnp.float32)  14.7 us
    gather x1, local copies, waits for them, and re-layouts, on_device(): jnp.take(mixed, perm_rows, axis=0) * scale_rows[:, None]  13.7 us
    dot_general x2, matrix products, on_device(): lax.dot_general(left_half, mixed, (((0,), (0,)), ((), ())), preferred_ele...  12.6 us
  transfers between devices with their start and end apart: 5, of which 5 were waited for; matrix products, arithmetic and copies ran while one was open for 11% of the time, Pallas kernels for 0%

commit v1 on v0

--- a/solution.py
+++ b/solution.py
@@ -19,8 +19,13 @@
 
 
 def spread(x, axis, root):
+
+    def spans_track(here_x, axis_tag):
+        carry_in = jnp.sum(lax.all_gather(here_x, axis_tag), axis=0)
+        return carry_in
+
     mine = lax.axis_index(axis) == root
-    return lax.psum(jnp.where(mine, x, jnp.zeros_like(x)), axis)
+    return spans_track(jnp.where(mine, x, jnp.zeros_like(x)), axis)
 
 
 def on_device(sim, diag_blocks, match_perm, match_scale, features):

time: 505 us -> 850 us (1.68)
  waiting for transfers between devices: 375 us -> 684 us
  other arithmetic: 35.4 us -> 70.7 us
    all_gather x0 -> x2, waiting for transfers between devices: none -> 261 us  [spans_track(): carry_in = jnp.sum(lax.all_gather(here_x, axis_tag), axis=0)]
    ppermute x2, waiting for transfers between devices: 285 us -> 382 us  [shifted(): return lax.ppermute(value, axis, pairs)]
    psum x1 -> x0, waiting for transfers between devices: 44.8 us -> none  [spread(): return lax.psum(jnp.where(mine, x, jnp.zeros_like(x)), axis)]
    reduce_sum x0 -> x2, other arithmetic: none -> 32.4 us  [spans_track(): carry_in = jnp.sum(lax.all_gather(here_x, axis_tag), axis=0)]
  transfers between devices with their start and end apart: 5 -> 6, of which waited for: 5 -> 4; matrix products, arithmetic and copies ran while one was open for 11% -> 15% of each run, Pallas kernels for 0% -> 0%
where the time goes in v1:
time: 850 us
  waiting for transfers between devices  684 us (80%)
  other arithmetic  70.7 us (8%)
  local copies, waits for them, and re-layouts  43.6 us (5%)
  matrix products  30 us (4%)
  between operations  13.9 us (2%)
    ppermute x2, waiting for transfers between devices, shifted(): return lax.ppermute(value, axis, pairs)  382 us
    all_gather x2, waiting for transfers between devices, spans_track(): carry_in = jnp.sum(lax.all_gather(here_x, axis_tag), axis=0)  261 us
    reduce_scatter x1, waiting for transfers between devices, on_device(): lax.psum_scatter(partial_value, 'col', scatter_dimension=0, tiled=True)  34.4 us
    reduce_sum x2, other arithmetic, spans_track(): carry_in = jnp.sum(lax.all_gather(here_x, axis_tag), axis=0)  32.4 us
    gather x2, local copies, waits for them, and re-layouts, on_device(): jnp.take(whole_block, own_perm, axis=1) * own_scale[None, :]  19.8 us
  transfers between devices with their start and end apart: 6, of which 4 were waited for; matrix products, arithmetic and copies ran while one was open for 15% of the time, Pallas kernels for 0%

profile of v1, /device:TPU:0, one launch (start us, length us, event | category | flops | bytes accessed | tf_op | source)
XLA Modules:
  0.0 849.6 jit_solution(15762607525282985172)
XLA Ops:
  7.2 0.0 copy-start
  7.2 0.0 all-gather.7.cloned.1.call-start
  7.2 6.2 broadcast_select_fusion.3
  13.4 0.0 all-gather.7.cloned.1.call-update
  13.4 0.0 all-gather.5.cloned.1.call-start
  13.5 0.7 all-gather.5.cloned.1.call-update
  14.2 0.0 reduce-scatter.2.cloned.1.call-start
  14.2 6.5 copy.12
  20.7 0.5 collective-permute-start
  21.2 0.8 dynamic_slice.23
  22.0 0.8 compare_select_fusion.1
  22.9 5.5 collective-permute-done
  28.4 8.2 broadcast_select_fusion.2
  36.6 8.3 pad_maximum_fusion
  44.9 13.3 %gather_fusion = bf16[1024,2048]{1,0:T(8,128)(2,1)} fusion(bf16[2048,2048]{0,1:T(8,128)(2,1)} %pad_maximum_fusion, s32[1024]{0:T(1024)S(1)} %broadcast_clamp_fusion.1), kind=kCustom, calls=%fused_computation | custom fusion | bytes 8392704 | tf_op jit(solution)/shard_map/jit(_take)/gather | solution.py:49
  58.3 6.4 copy.14
  64.7 5.6 fusion.3
  70.3 5.4 collective-permute-start.1
  75.7 0.8 constant_dynamic-slice_fusion
  76.5 0.8 compare_select_fusion
  77.3 382.2 %collective-permute-done.1 = bf16[2048,1024]{1,0:T(8,128)(2,1)} collective-permute-done((bf16[2048,1024]{1,0:T(8,128)(2,1)}, bf16[2048,1024]{1,0:T(8,128)(2,1)}, u32[]{:S(2)}, u32[]{:S(2)}) %collective-permute-start.1) | collective-permute-done | bytes 4194336 | tf_op jit(solution)/shard_map/ppermute | solution.py:18
  459.4 15.0 %add_convert_fusion = bf16[2048,1024]{1,0:T(8,128)(2,1)} fusion(bf16[2048,1024]{1,0:T(8,128)(2,1)} %collective-permute-done.1, bf16[2048,1024]{1,0:T(8,128)(2,1)} %param.6, bf16[2048,1024]{0,1:T(8,128)(2,1)} %get-tuple-element.7, bf16[2048,1024]{0,1:T(8,128)(2,1)} %get-tuple-element.6), kind=kOutput, calls=%fused_computation.9 | convolution fusion | flops 8613003264 | bytes 20971520 | tf_op jit(solution)/shard_map/dot_general | solution.py:52
  474.4 13.7 %gather_fusion.1 = bf16[2048,1024]{1,0:T(8,128)(2,1)} fusion(bf16[2048,1024]{1,0:T(8,128)(2,1)} %add_convert_fusion, s32[2048]{0:T(1024)S(1)} %broadcast_clamp_fusion), kind=kCustom, calls=%fused_computation.1 | custom fusion | bytes 8396800 | tf_op jit(solution)/shard_map/jit(_take)/gather | solution.py:58
  488.2 4.3 multiply_convert_fusion.1
  492.5 1.6 collective-permute-start.2
  494.0 0.0 all-gather.7.cloned.1.call-done
  494.1 18.2 %reduce_sum.25 = bf16[2048,1024]{1,0:T(8,128)(2,1)} reduce(bf16[8,2048,1024]{2,1,0:T(8,128)(2,1)} %bitcast.21, bf16[]{:T(256)} %constant.100.clone.1), dimensions={0}, to_apply=%region_1.2 | reduce | flops 14680064 | bytes 37748736 | tf_op jit(solution)/shard_map/reduce_sum | solution.py:24
  512.2 261.1 %all-gather.5.cloned.1.call-done = bf16[16384,1024]{1,0:T(8,128)(2,1)} async-done(((bf16[2048,1024]{1,0:T(8,128)(2,1)}), bf16[16384,1024]{1,0:T(8,128)(2,1)}) %all-gather.5.cloned.1.call-update) | async-done | bytes 33554448 | tf_op jit(solution)/shard_map/all_gather | solution.py:24
  773.3 14.2 %reduce_sum.24 = bf16[2048,1024]{1,0:T(8,128)(2,1)} reduce(bf16[8,2048,1024]{2,1,0:T(8,128)(2,1)} %bitcast.22, bf16[]{:T(256)} %constant.100.clone.1), dimensions={0}, to_apply=%region_0.1 | reduce | flops 14680064 | bytes 37748736 | tf_op jit(solution)/shard_map/reduce_sum | solution.py:24
  787.5 0.0 copy-start.1
  787.5 0.0 copy-start.2
  787.5 7.7 fusion.5
  795.2 0.0 copy-done.1
  795.3 0.0 copy-done.2
  795.3 4.6 fusion.4
  799.9 0.0 collective-permute-done.2
  799.9 4.1 fusion.2
  804.0 0.0 copy-start.3
  804.0 2.0 copy-done.3
  806.0 0.0 copy-done
  806.1 2.6 fusion.6
  808.7 0.0 reduce-scatter.2.cloned.1.call-update
  808.7 34.4 %reduce-scatter.2.cloned.1.call-done = f32[256,256]{1,0:T(8,128)} async-done(((f32[2048,256]{1,0:T(8,128)}), f32[256,256]{1,0:T(8,128)}) %reduce-scatter.2.cloned.1.call-update) | async-done | bytes 262160 | tf_op jit(solution)/shard_map/reduce_scatter | solution.py:76
  (6 shorter events, 0.0 us)
Async XLA Ops:
  7.2 798.9 %copy-start = (bf16[1024,256]{1,0:T(8,128)(2,1)S(1)}, bf16[1024,256]{1,0:T(8,128)(2,1)}, u32[]{:S(2)}) copy-start(bf16[1024,256]{1,0:T(8,128)(2,1)} %param.9) | copy-start | bytes 1572868
  7.2 486.9 %all-gather.7.cloned.1.call-start = ((), (), s32[]{:S(2)}) async-start(), calls=%async_computation.3 | async-start | bytes 37748736 | tf_op jit(solution)/shard_map/all_gather | solution.py:24
  13.4 759.9 %all-gather.5.cloned.1.call-start = ((), (), s32[]{:S(2)}) async-start(), calls=%async_computation.2 | async-start | bytes 37748736 | tf_op jit(solution)/shard_map/all_gather | solution.py:24
  14.2 828.9 %reduce-scatter.2.cloned.1.call-start = ((), (), s32[]{:S(2)}) async-start(), calls=%async_computation.1 | async-start | bytes 2359296 | tf_op jit(solution)/shard_map/reduce_scatter | solution.py:76
  20.7 7.6 collective-permute-start
  70.3 389.2 %collective-permute-start.1 = (bf16[2048,1024]{1,0:T(8,128)(2,1)}, bf16[2048,1024]{1,0:T(8,128)(2,1)}, u32[]{:S(2)}, u32[]{:S(2)}) collective-permute-start(bf16[2048,1024]{1,0:T(8,128)(2,1)} %fusion.3), channel_id=1, source_target_pairs={{0,4},{1,5},{2,6},{3,7},{4,0},{5,1},{6,2},{7,3},{8,12},{9,13},{10,... | collective-permute-start | bytes 12582920 | tf_op jit(solution)/shard_map/ppermute | solution.py:18
  492.5 307.5 %collective-permute-start.2 = (bf16[2048,1024]{1,0:T(8,128)(2,1)}, bf16[2048,1024]{1,0:T(8,128)(2,1)}, u32[]{:S(2)}, u32[]{:S(2)}) collective-permute-start(bf16[2048,1024]{1,0:T(8,128)(2,1)} %multiply_convert_fusion.1), channel_id=1, source_target_pairs={{0,16},{8,24},{16,0},{24,8},{1,17},{9,25},{17,1},{25,9},{2,18},{10... | collective-permute-start | bytes 12582920 | tf_op jit(solution)/shard_map/ppermute | solution.py:18
  787.5 7.7 copy-start.1
  787.5 7.7 copy-start.2
  804.0 2.0 copy-start.3
Sparse Core Ops, SparseCore 0:
  13.5 470.7 all-gather.6
  486.5 286.7 all-gather.4
  808.8 34.2 reduce-scatter.1
